TPU v7x, 32 devices: a whole 2x2x4 slice. The times are simulated.
32 devices in a mesh: wave: 4 (over y, core), lev: 8 (over z, x).
Axes of the slice: x: 2, y: 2, z: 4, core: 2. Of those that a mesh axis runs over, the one named last changes fastest.
Arguments:
- spectral: bfloat16 [8, 6, 1280, 1280], P('lev', None, 'wave'), may hold values from -0.16992188 to 0.16992188
- legendre: bfloat16 [1280, 6, 1280], P('wave'), may hold values from -0.15625 to 0.15625
- slot_wave: int32 [1280], replicated, may hold values from 0 to 1279, each once
- cycle_len: int32 [6], replicated, may hold values from 2576 to 5136, as said below
- lat_order: int32 [12], replicated, may hold values from 0 to 11, each once
Outputs:
- grid: float32 [12, 124416], P('wave', 'lev')
Inputs may be any that keep to these rules, and one draw needn't show every extreme that they name: `slot_wave`: each wavenumber is held in exactly one slot. `lat_order`: each latitude is held in exactly one row. `cycle_len`: every cycle length is a multiple of 16; some pair has exactly 5136 points and some pair exactly 2576.
All inputs are finite; a program needn't handle non-finite values.
Results may differ from a plain program's by a relative error of at most 0.0003.
Values sent between devices are 32-bit elements; how exact they have to be, the bound alone decides.
A program may use at most 64 MiB of HBM per device.

v0:
```python
import math

import jax
import jax.numpy as jnp
from jax import lax
from jax.sharding import PartitionSpec as P

MMAX = 1280
NDEG = 1280
RMAX = 5136
FIELDS = 3


def local(spectral, legendre, slot_wave, cycle_len, lat_order):
    slot_count = spectral.shape[2]
    half_cycles = legendre.shape[1]
    wave_index = lax.axis_index("wave")
    lev_count = lax.axis_size("lev")
    padded_len = (RMAX + 8 * lev_count - 1) // (8 * lev_count) * 8 * lev_count
    points_dev = padded_len // lev_count
    local_waves = lax.dynamic_slice_in_dim(slot_wave, wave_index * slot_count, slot_count)
    degree = jnp.arange(NDEG, dtype=jnp.int32)
    live_mask = degree[None, :] >= local_waves[:, None]
    even_mask = (degree[None, :] + local_waves[:, None]) % 2 == 0
    nothing = jnp.zeros_like(spectral)
    even_part = jnp.where((live_mask & even_mask)[None, None], spectral, nothing)
    odd_part = jnp.where((live_mask & jnp.logical_not(even_mask))[None, None], spectral, nothing)
    stacked = jnp.stack([even_part, odd_part])
    halves = jnp.einsum("pxcsn,skn->pxcsk", stacked, legendre, preferred_element_type=jnp.float32)
    fourier = jnp.concatenate([halves[0] + halves[1], halves[0] - halves[1]], axis=3)
    ordered = jnp.take(fourier, lat_order, axis=3)
    fourier_all = lax.all_to_all(ordered, "wave", split_axis=3, concat_axis=2, tiled=True)
    cycle_count = fourier_all.shape[3]
    slots = jnp.arange(MMAX, dtype=jnp.int32)
    matches = slot_wave[:, None] == slots[None, :]
    inverse = jnp.sum(jnp.where(matches, slots[:, None], 0), axis=0)
    fourier_m = jnp.take(fourier_all, inverse, axis=2)
    rows = wave_index * cycle_count + jnp.arange(cycle_count, dtype=jnp.int32)
    latitudes = jnp.take(lat_order, rows)
    pairs = latitudes % half_cycles
    pair_match = pairs[:, None] == jnp.arange(half_cycles, dtype=jnp.int32)[None, :]
    lengths = jnp.sum(jnp.where(pair_match, cycle_len[None, :], 0), axis=1)
    points = lax.axis_index("lev") * points_dev + jnp.arange(points_dev, dtype=jnp.int32)
    waves = jnp.arange(MMAX, dtype=jnp.int32)
    phases = waves[None, :, None] * points[None, None, :] % lengths[:, None, None]
    angles = 2.0 * math.pi * phases.astype(jnp.float32) / lengths.astype(jnp.float32)[:, None, None]
    weights = jnp.where(waves == 0, 1.0, 2.0).astype(jnp.float32)[None, :, None]
    cosine = weights * jnp.cos(angles)
    sine = weights * jnp.sin(angles)
    valid = points[None, :] < lengths[:, None]
    piece = lax.all_gather(fourier_m, "lev", axis=0, tiled=True)
    count = piece.shape[0]
    coeffs = piece.reshape(count, FIELDS, 2, MMAX, cycle_count)
    highest = lax.Precision.HIGHEST
    result = jnp.einsum("lfmr,rmj->rjlf", coeffs[:, :, 0], cosine, precision=highest) - jnp.einsum(
        "lfmr,rmj->rjlf", coeffs[:, :, 1], sine, precision=highest
    )
    result = jnp.where(valid[:, :, None, None], result, jnp.float32(0.0))
    columns = result.reshape(cycle_count, points_dev, count * FIELDS)
    grid = columns.reshape(cycle_count, points_dev * columns.shape[2])
    return grid


def solution(mesh):
    in_specs = (P("lev", None, "wave", None), P("wave", None, None), P(), P(), P())
    out_specs = P("wave", "lev")
    return jax.shard_map(local, mesh=mesh, in_specs=in_specs, out_specs=out_specs, check_vma=False)
```

profile of v0, /device:TPU:0, one launch (start us, length us, event | category | flops | bytes accessed | tf_op | source)
XLA Modules:
  0.0 410.1 jit_solution(444186750456901210)
XLA Ops:
  0.0 0.8 dynamic_slice.3
  0.8 1.3 fusion.31
  2.1 8.6 %fusion.16 = (bf16[1,1,6,320,1280]{4,2,0,3,1:T(8,128)(2,1)S(1)}, bf16[1,1,6,320,1280]{4,2,0,3,1:T(8,128)(2,1)S(1)}) fusion(bf16[1,6,320,1280]{3,2,1,0:T(8,128)(2,1)} %param.5, pred[320,1280]{1,0:T(8,128)(4,1)S(1)} %get-tuple-element.9, pred[320,1280]{1,0:T(8,128)(4,1)S(1)} %get-tuple-element.10), kind=kLoop, calls=%fused_computation.26 | loop fusion | flops 4915200 | bytes 15564800 | tf_op jit(solution)/shard_map/stack | solution.py:28
  10.6 11.0 %fusion.23 = f32[2,1,6,320,6]{4,2,0,3,1:T(8,128)S(1)} fusion(bf16[320,6,1280,1]{2,0,1,3:T(8,128)(2,1)} %bitcast.78, bf16[1,1,6,320,1280]{4,2,0,3,1:T(8,128)(2,1)S(1)} %get-tuple-element.6, bf16[1,1,6,320,1280]{4,2,0,3,1:T(8,128)(2,1)S(1)} %get-tuple-element.5), kind=kOutput, calls=%fused_computation.38 | convolution fusion | flops 63897600 | bytes 14837760 | tf_op jit(solution)/shard_map/pxcsn,skn->pxcsk/dot_general | solution.py:29
  21.6 0.0 copy-start
  21.6 0.2 fusion.33
  21.8 0.2 subtract_bitcast_fusion
  21.9 0.3 copy-done
  22.3 0.0 copy-start.2
  22.3 0.4 maximum_bitcast_fusion.4
  22.7 0.0 copy-start.3
  22.7 0.6 copy.51
  23.3 0.6 gather_fusion.1
  23.9 0.1 bitcast_select_fusion.1
  23.9 0.8 copy.52
  24.7 4.5 %all-to-all-start = ((f32[1,6,320,12]{2,0,1,3:T(1,128)}), f32[1,6,320,12]{2,0,1,3:T(1,128)S(1)}, u32[]{:S(2)}, u32[]{:S(2)}) async-start(f32[1,6,320,12]{2,0,1,3:T(1,128)} %copy.52), calls=%async_computation | async-start | bytes 221184 | tf_op jit(solution)/shard_map/all_to_all | solution.py:32
  29.2 0.0 copy-done.2
  29.2 0.7 select_reduce_fusion
  30.0 0.6 gather_fusion
  30.7 0.0 copy-done.3
  30.7 0.2 select_reduce_fusion.1
  30.9 0.0 copy-start.4
  30.9 0.0 copy-start.5
  31.0 2.0 iota_multiply_fusion
  32.9 0.1 broadcast_compare_fusion
  33.0 0.6 all-to-all-done
  33.6 0.1 copy.53
  33.6 2.0 copy.66
  35.7 4.7 %gather_fusion.2 = f32[1280,6,3]{1,2,0:T(4,128)S(1)} fusion(f32[6,1280,3]{0,2,1:T(4,128)} %bitcast.75, s32[2048]{0:T(1024)S(1)} %pad_clamp_fusion), kind=kCustom, calls=%fused_computation.2 | custom fusion | bytes 189440 | tf_op jit(solution)/shard_map/jit(_take)/gather | solution.py:37
  40.4 5.6 %bitcast_select_fusion = f32[1,6,1280,3]{1,3,2,0:T(4,128)} fusion(f32[1280,6,3]{1,2,0:T(4,128)S(1)} %gather_fusion.2, pred[1280]{0:T(1024)(128)(4,1)S(1)} %compare_and_fusion), kind=kLoop, calls=%fused_computation.34 | loop fusion | flops 23040 | bytes 185600 | tf_op jit(solution)/shard_map/jit(_take)/select_n | solution.py:37
  46.1 0.0 copy-start.1
  46.1 2.2 copy.56
  48.2 33.4 %all_gather.3 = f32[8,6,1280,3]{2,1,3,0:T(8,128)S(1)} all-gather(f32[1,6,1280,3]{2,1,3,0:T(8,128)S(1)} %copy.56), channel_id=1, replica_groups=mesh['wave'=4,'lev'=8] {'lev'}, dimensions={0}, use_global_device_ids=true | all-gather | bytes 829440 | tf_op jit(solution)/shard_map/all_gather | solution.py:51
  81.7 0.2 copy.57
  81.9 0.1 fusion.48
  82.0 0.0 copy-done.4
  82.0 0.0 copy-done.5
  82.0 0.0 copy-done.1
  82.0 175.0 %fusion.6 = f32[3,648,8,3]{1,2,3,0:T(8,128)S(1)} fusion(f32[1280]{0:T(1024)S(1)} %fusion.40, f32[3]{0:T(128)S(1)} %get-tuple-element.12, s32[3]{0:T(128)S(1)} %get-tuple-element.11, s32[1280,648]{0,1:T(8,128)S(1)} %copy-done.1, pred[3]{0:T(512)(128)(4,1)S(1)} %broadcast_compare_fusion.1, f32[8,3,1,1280,3]{3,0,4,2,1:T(8,128)S(1)} %get-tuple-element.8), kind=kOutput, calls=%fused_computation.14 | convolution fusion | flops 744007680 | bytes 3878171 | tf_op jit(solution)/shard_map/lfmr,rmj->rjlf/dot_general | solution.py:55
  257.0 137.6 %fusion.37 = f32[3,648,8,3]{1,2,3,0:T(8,128)S(1)} fusion(f32[3,648,8,3]{1,2,3,0:T(8,128)S(1)} %fusion.6, f32[1280]{0:T(1024)S(1)} %fusion.40, f32[3]{0:T(128)} %copy-done.4, pred[3]{0:T(512)(128)(4,1)} %copy-done.5, s32[3]{0:T(128)S(1)} %get-tuple-element.11, s32[1280,648]{0,1:T(8,128)S(1)} %copy-done.1, f32[8,3,1,1280,3]{3,0,4,2,1:T(8,128)S(1)} %get-tuple-element.7, ...), kind=kOutput, calls=%fused_computation.52 | convolution fusion | flops 744100992 | bytes 4066739 | tf_op jit(solution)/shard_map/lfmr,rmj->rjlf/dot_general | solution.py:55
  394.6 4.7 %copy.60 = f32[3,648,8,3]{3,2,1,0:T(8,128)} copy(f32[3,648,8,3]{1,2,3,0:T(8,128)S(1)} %fusion.37) | data formatting | bytes 373248 | tf_op jit(solution)/shard_map/jit(_where)/select_n | solution.py:58
  399.4 10.3 %reshape_reshape.3 = f32[3,15552]{1,0:T(4,128)} reshape(f32[3,648,8,3]{3,2,1,0:T(8,128)} %copy.60) | data formatting | bytes 373248 | tf_op jit(solution)/shard_map/reshape;reshape | solution.py:60
  (13 shorter events, 0.1 us)
Async XLA Ops:
  21.6 0.7 copy-start
  22.3 7.0 %copy-start.2 = (s32[1280]{0:T(1024)S(1)}, s32[1280]{0:T(1024)}, u32[]{:S(2)}) copy-start(s32[1280]{0:T(1024)} %param.7) | copy-start | bytes 15364
  22.7 8.0 %copy-start.3 = (s32[6]{0:T(128)S(1)}, s32[6]{0:T(128)}, u32[]{:S(2)}) copy-start(s32[6]{0:T(128)} %param.8) | copy-start | bytes 76
  24.7 8.9 %all-to-all-start = ((f32[1,6,320,12]{2,0,1,3:T(1,128)}), f32[1,6,320,12]{2,0,1,3:T(1,128)S(1)}, u32[]{:S(2)}, u32[]{:S(2)}) async-start(f32[1,6,320,12]{2,0,1,3:T(1,128)} %copy.52), calls=%async_computation | async-start | bytes 221184 | tf_op jit(solution)/shard_map/all_to_all | solution.py:32
  30.9 51.1 %copy-start.4 = (f32[3]{0:T(128)}, f32[3]{0:T(128)S(1)}, u32[]{:S(2)}) copy-start(f32[3]{0:T(128)S(1)} %get-tuple-element.12) | copy-start | bytes 40
  30.9 51.1 %copy-start.5 = (pred[3]{0:T(512)(128)(4,1)}, pred[3]{0:T(512)(128)(4,1)S(1)}, u32[]{:S(2)}) copy-start(pred[3]{0:T(512)(128)(4,1)S(1)} %broadcast_compare_fusion.1) | copy-start | bytes 13
  46.1 35.9 %copy-start.1 = (s32[1280,648]{0,1:T(8,128)S(1)}, s32[1280,648]{0,1:T(8,128)}, u32[]{:S(2)}) copy-start(s32[1280,648]{0,1:T(8,128)} %iota_multiply_fusion) | copy-start | bytes 9953284
where the time goes:
time: 416 us; the launch traced here: 410 us
  matrix products  324 us (78%)
  blocking collectives  33.4 us (8%)
  local copies, waits for them, and re-layouts  28 us (7%)
  other arithmetic  19.3 us (5%)
  starting transfers between devices  4.52 us (1%)
    dot_general x1, matrix products, local(): jnp.einsum('lfmr,rmj->rjlf', coeffs[:, :, 1], sine, precision=highest)  175 us
    dot_general x1, matrix products, local(): jnp.einsum('lfmr,rmj->rjlf', coeffs[:, :, 0], cosine, precision=highest)  138 us
    all_gather x1, blocking collectives, local(): piece = lax.all_gather(fourier_m, 'lev', axis=0, tiled=True)  33.4 us
    dot_general x1, matrix products, local(): jnp.einsum('pxcsn,skn->pxcsk', stacked, legendre, preferred_element_type=...  11 us
    another operation x1, local copies, waits for them, and re-layouts, local(): grid = columns.reshape(cycle_count, points_dev * columns.shape[2])  10.3 us
    another operation x1, other arithmetic, local(): stacked = jnp.stack([even_part, odd_part])  8.55 us
  transfers between devices with their start and end apart: 1, of which 1 were waited for; matrix products, arithmetic and copies ran while one was open for 1% of the time, Pallas kernels for 0%

commit v1 on v0

v1 whole, which is shorter than its diff:
```python
import functools
import math

import jax
import jax.numpy as jnp
from jax import lax
from jax.experimental import pallas as pl
from jax.experimental.pallas import tpu as pltpu
from jax.sharding import PartitionSpec as P

RMAX = 5136
FIELDS = 3


def split(value):
    high = value.astype(jnp.bfloat16)
    return high, (value - high.astype(jnp.float32)).astype(jnp.bfloat16)


def dot_nt(left, right):
    return lax.dot_general(left, right, (((1,), (1,)), ((), ())), preferred_element_type=jnp.float32)


def turns(t):
    y = math.pi * t
    z = y * y
    sine = jnp.full_like(z, 1.0 / math.factorial(13))
    for n in (11, 9, 7, 5, 3, 1):
        sign = -1.0 if (n // 2) % 2 else 1.0
        sine = sine * z + sign / math.factorial(n)
    sine = sine * y
    cosine = jnp.full_like(z, 1.0 / math.factorial(12))
    for n in (10, 8, 6, 4, 2, 0):
        sign = -1.0 if (n // 2) % 2 else 1.0
        cosine = cosine * z + sign / math.factorial(n)
    return 1.0 - 2.0 * sine * sine, 2.0 * sine * cosine


def synth_kernel(step, step_pad, rows_dev, len_ref, inv_ref, wave_ref, coef_ref, out_ref, e_ref, w_ref, t_ref):
    lev_count = out_ref.shape[0]
    cycles, parts, slots = coef_ref.shape
    fields = parts // 2
    row_count = rows_dev * lev_count
    waves = wave_ref[...]
    weights = jnp.where(waves == 0.0, 1.0, 2.0)
    index = lax.broadcasted_iota(jnp.int32, (48, 1), 0)
    mult = jnp.where(
        index < 8,
        index,
        jnp.where(index < 24, 8 * (index - 8), jnp.where(index < 32, step * (index - 24), 8 * step * (index - 32))),
    ).astype(jnp.float32)
    products = waves * mult
    for r in range(cycles):
        length = len_ref[r]
        inverse = inv_ref[r]
        whole = jnp.floor(products * inverse + 0.5)
        cosine, sine = turns((products - whole * length) * inverse)
        for k in range(step_pad // 8):
            c0, s0, c1, s1 = cosine[0:8], sine[0:8], cosine[8 + k : 9 + k], sine[8 + k : 9 + k]
            e_ref[0, 8 * k : 8 * k + 8] = c0 * c1 - s0 * s1
            e_ref[1, 8 * k : 8 * k + 8] = s0 * c1 + c0 * s1
        for k in range((row_count + 15) // 16):
            tc, ts = [], []
            for h in (2 * k, 2 * k + 1):
                c0, s0, c1, s1 = cosine[24:32], sine[24:32], cosine[32 + h : 33 + h], sine[32 + h : 33 + h]
                tc.append(c0 * c1 - s0 * s1)
                ts.append(s0 * c1 + c0 * s1)
            for place, value in ((0, tc), (slots, ts)):
                high, low = split(jnp.concatenate(value, axis=0))
                t_ref[0, 16 * k : 16 * k + 16, place : place + slots] = high
                t_ref[1, 16 * k : 16 * k + 16, place : place + slots] = low
        for f in range(fields):
            real = coef_ref[r, 2 * f : 2 * f + 1] * weights
            imag = coef_ref[r, 2 * f + 1 : 2 * f + 2] * weights
            for k in range(step_pad // 16):
                ec = e_ref[0, 16 * k : 16 * k + 16]
                es = e_ref[1, 16 * k : 16 * k + 16]
                at = f * step_pad + 16 * k
                for place, value in ((0, real * ec - imag * es), (slots, -(real * es + imag * ec))):
                    high, low = split(value)
                    w_ref[0, at : at + 16, place : place + slots] = high
                    w_ref[1, at : at + 16, place : place + slots] = low
        total = dot_nt(t_ref[0], w_ref[0]) + dot_nt(t_ref[0], w_ref[1]) + dot_nt(t_ref[1], w_ref[0])
        shape = total.shape
        point = lax.broadcasted_iota(jnp.int32, shape, 0) * step + lax.broadcasted_iota(jnp.int32, shape, 1) % step_pad
        total = jnp.where(point.astype(jnp.float32) < length, total, 0.0)
        for d in range(lev_count):
            out_ref[d, r * rows_dev : (r + 1) * rows_dev] = total[d * rows_dev : (d + 1) * rows_dev]
    used = cycles * rows_dev
    if used < out_ref.shape[1]:
        out_ref[:, used:] = jnp.zeros((lev_count, out_ref.shape[1] - used, out_ref.shape[2]), jnp.float32)


def place_kernel(step, step_pad, rows_dev, cycles, x_ref, out_ref):
    lev_count, rows, width = x_ref.shape
    fields = width // step_pad
    group = lev_count * fields
    span = step * group
    span_pad = (span + 127) // 128 * 128
    source = lax.broadcasted_iota(jnp.int32, (width, 1), 0)
    shift = source % step_pad
    target = jnp.where(shift < step, shift * group + source // step_pad, -1)
    lane = lax.broadcasted_iota(jnp.int32, (width, span_pad), 1)
    chosen = jnp.where(lane == target, 1.0, 0.0).astype(jnp.bfloat16)
    values = x_ref[...].reshape(lev_count * rows, width)
    high, low = split(values)
    spread = jnp.dot(high, chosen, preferred_element_type=jnp.float32) + jnp.dot(
        low, chosen, preferred_element_type=jnp.float32
    )
    total = spread[:rows]
    for level in range(1, lev_count):
        total = total + pltpu.roll(spread[level * rows : (level + 1) * rows], fields * level, 1)
    for r in range(cycles):
        for q in range(rows_dev):
            row = r * rows_dev + q
            out_ref[r : r + 1, q * span : (q + 1) * span] = total[row : row + 1, :span]


def legendre_kernel(wave_ref, spec_ref, leg_ref, out_ref):
    parts, block, degrees = spec_ref.shape
    half_cycles = leg_ref.shape[0]
    table = leg_ref[...].reshape(half_cycles * block, degrees)
    waves = wave_ref[0]
    degree = lax.broadcasted_iota(jnp.int32, (block, degrees), 1)
    live = degree >= waves
    parity = (degree + waves) & 1
    even = (live & (parity == 0))[None]
    odd = (live & (parity == 1))[None]
    values = spec_ref[...].astype(jnp.float32)
    cells = parts * block
    shape = (half_cycles, block, cells)
    own = lax.broadcasted_iota(jnp.int32, shape, 1) == lax.broadcasted_iota(jnp.int32, shape, 2) % block
    sums = []
    for mask in (even, odd):
        part = jnp.where(mask, values, 0.0).reshape(cells, degrees).astype(jnp.bfloat16)
        product = dot_nt(table, part).reshape(shape)
        sums.append(jnp.sum(jnp.where(own, product, 0.0), axis=1))
    out_ref[0, 0] = sums[0] + sums[1]
    out_ref[0, 1] = sums[0] - sums[1]


def exchange_kernel(x_ref, out_ref, own_sem, send_sem, recv_sem):
    count = x_ref.shape[0]
    me = lax.axis_index("lev")
    barrier = pltpu.get_barrier_semaphore()
    for offset in range(1, count):
        peer = lax.rem(me + offset, count)
        pl.semaphore_signal(barrier, inc=1, device_id={"lev": peer}, device_id_type=pl.DeviceIdType.MESH)
    kept = pltpu.make_async_copy(x_ref.at[me], out_ref.at[me], own_sem)
    kept.start()
    pl.semaphore_wait(barrier, count - 1)
    copies = []
    for offset in range(1, count):
        peer = lax.rem(me + offset, count)
        copy = pltpu.make_async_remote_copy(
            src_ref=x_ref.at[peer],
            dst_ref=out_ref.at[me],
            send_sem=send_sem.at[offset],
            recv_sem=recv_sem.at[offset],
            device_id={"lev": peer},
            device_id_type=pl.DeviceIdType.MESH,
        )
        copy.start()
        copies.append(copy)
    kept.wait()
    for copy in copies:
        copy.wait()


def local(spectral, legendre, slot_wave, cycle_len, lat_order):
    slot_count = spectral.shape[2]
    degrees = spectral.shape[3]
    half_cycles = legendre.shape[1]
    wave_index = lax.axis_index("wave")
    lev_count = lax.axis_size("lev")
    wave_count = lax.axis_size("wave")
    slots = slot_wave.shape[0]
    padded_len = (RMAX + 8 * lev_count - 1) // (8 * lev_count) * 8 * lev_count
    points_dev = padded_len // lev_count
    step = max(b for b in range(8, 80, 8) if points_dev % b == 0)
    step_pad = (step + 15) // 16 * 16
    rows_dev = points_dev // step
    row_count = rows_dev * lev_count
    parts = spectral.shape[0] * spectral.shape[1]
    cycle_count = lat_order.shape[0] // wave_count

    local_waves = lax.dynamic_slice_in_dim(slot_wave, wave_index * slot_count, slot_count)
    block = 32 if slot_count % 32 == 0 else 16
    blocks = slot_count // block
    cells = parts * block
    fourier = pl.pallas_call(
        legendre_kernel,
        grid=(blocks,),
        out_shape=jax.ShapeDtypeStruct((blocks, 2, half_cycles, cells), jnp.float32),
        in_specs=[
            pl.BlockSpec((1, block, 1), lambda i: (i, 0, 0)),
            pl.BlockSpec((parts, block, degrees), lambda i: (0, i, 0)),
            pl.BlockSpec((half_cycles, block, degrees), lambda i: (0, i, 0)),
        ],
        out_specs=pl.BlockSpec((1, 2, half_cycles, cells), lambda i: (i, 0, 0, 0)),
        name="legendre",
    )(local_waves.reshape(blocks, block, 1), spectral.reshape(parts, slot_count, degrees), jnp.transpose(legendre, (1, 0, 2)))
    fourier = fourier.reshape(blocks, 2 * half_cycles, parts, block)
    fourier = jnp.transpose(fourier, (1, 2, 0, 3)).reshape(2 * half_cycles, parts * slot_count)
    ordered = jnp.take(fourier, lat_order, axis=0)
    ordered = ordered.reshape(wave_count, cycle_count, parts, slot_count)
    shared = lax.all_to_all(ordered, "wave", split_axis=0, concat_axis=0, tiled=True)
    coeffs = jnp.transpose(shared, (1, 2, 0, 3)).reshape(cycle_count, parts, slots)

    rows = wave_index * cycle_count + jnp.arange(cycle_count, dtype=jnp.int32)
    pairs = jnp.take(lat_order, rows) % half_cycles
    pair_match = pairs[:, None] == jnp.arange(half_cycles, dtype=jnp.int32)[None, :]
    lengths = jnp.sum(jnp.where(pair_match, cycle_len[None, :], 0), axis=1).astype(jnp.float32)
    waves = slot_wave.astype(jnp.float32)[None, :]
    send_rows = (cycle_count * rows_dev + 7) // 8 * 8
    width = parts // 2 * step_pad
    smem = pl.BlockSpec(memory_space=pltpu.SMEM)
    vmem = pl.BlockSpec(memory_space=pltpu.VMEM)
    row_pad = (row_count + 15) // 16 * 16
    points = pl.pallas_call(
        functools.partial(synth_kernel, step, step_pad, rows_dev),
        out_shape=jax.ShapeDtypeStruct((lev_count, send_rows, width), jnp.float32),
        in_specs=[smem, smem, vmem, vmem],
        out_specs=vmem,
        scratch_shapes=[
            pltpu.VMEM((2, step_pad, slots), jnp.float32),
            pltpu.VMEM((2, width, 2 * slots), jnp.bfloat16),
            pltpu.VMEM((2, row_pad, 2 * slots), jnp.bfloat16),
        ],
        name="synth",
    )(lengths, 1.0 / lengths, waves, coeffs)
    owned = pl.pallas_call(
        exchange_kernel,
        out_shape=jax.ShapeDtypeStruct(points.shape, jnp.float32),
        in_specs=[vmem],
        out_specs=vmem,
        scratch_shapes=[
            pltpu.SemaphoreType.DMA,
            pltpu.SemaphoreType.DMA((lev_count,)),
            pltpu.SemaphoreType.DMA((lev_count,)),
        ],
        compiler_params=pltpu.CompilerParams(collective_id=0, has_side_effects=True),
        name="exchange",
    )(points)
    return pl.pallas_call(
        functools.partial(place_kernel, step, step_pad, rows_dev, cycle_count),
        out_shape=jax.ShapeDtypeStruct((cycle_count, points_dev * lev_count * (parts // 2)), jnp.float32),
        in_specs=[vmem],
        out_specs=vmem,
        name="place",
    )(owned)


def solution(mesh):
    in_specs = (P("lev", None, "wave", None), P("wave", None, None), P(), P(), P())
    out_specs = P("wave", "lev")
    return jax.shard_map(local, mesh=mesh, in_specs=in_specs, out_specs=out_specs, check_vma=False)
```

time: 416 us -> 47.4 us (0.11); the launches traced: 410 us -> 46.8 us
  matrix products: 324 us -> 0 us
  blocking collectives: 33.4 us -> 0 us
  Pallas kernels: 0 us -> 31 us
  local copies, waits for them, and re-layouts: 28 us -> 5.94 us
  other arithmetic: 19.3 us -> 3.4 us
    dot_general x3 -> x0, matrix products: 324 us -> none  [the longest x1 175 us: local(): jnp.einsum('lfmr,rmj->rjlf', coeffs[:, :, 1], sine, precision=highest)]
    all_gather x1 -> x0, blocking collectives: 33.4 us -> none  [local(): piece = lax.all_gather(fourier_m, 'lev', axis=0, tiled=True)]
    pallas_call x0 -> x4, Pallas kernels: none -> 31 us  [the longest x1 11.1 us: local(): pl.pallas_call(exchange_kernel, out_shape=jax.ShapeDtypeStruct(points.sha...]
    another operation x1 -> x0, local copies, waits for them, and re-layouts: 10.3 us -> none  [local(): grid = columns.reshape(cycle_count, points_dev * columns.shape[2])]
    another operation x1 -> x0, other arithmetic: 8.55 us -> none  [local(): stacked = jnp.stack([even_part, odd_part])]
    select_n x3 -> x0, local copies, waits for them, and re-layouts: 7.65 us -> none  [the longest x1 4.72 us: local(): result = jnp.where(valid[:, :, None, None], result, jnp.float32(0.0))]
    gather x3, local copies, waits for them, and re-layouts: 5.95 us -> 1.33 us  [the longest x2 0.69 us: local(): ordered = jnp.take(fourier, lat_order, axis=0)]
    select_n x8 -> x4, other arithmetic: 5.76 us -> 1.43 us  [the longest x2 1.41 us: local(): ordered = jnp.take(fourier, lat_order, axis=0)]
  transfers between devices with their start and end apart: 1 -> 1, of which waited for: 1 -> 1; matrix products, arithmetic and copies ran while one was open for 1% -> 5% of each run, Pallas kernels for 0% -> 0%
where the time goes in v1:
time: 47.4 us; the launch traced here: 46.8 us
  Pallas kernels  31 us (65%)
  local copies, waits for them, and re-layouts  5.94 us (13%)
  starting transfers between devices  4.26 us (9%)
  other arithmetic  3.4 us (7%)
  waiting for transfers between devices  2.18 us (5%)
    pallas_call x1, Pallas kernels, local(): pl.pallas_call(exchange_kernel, out_shape=jax.ShapeDtypeStruct(points.sha...  11.1 us
    pallas_call x1, Pallas kernels, local(): pl.pallas_call(legendre_kernel, grid=(blocks,), out_shape=jax.ShapeDtypeS...  10.1 us
    pallas_call x1, Pallas kernels, local(): pl.pallas_call(functools.partial(synth_kernel, step, step_pad, rows_dev),...  6.97 us
    all_to_all x1, starting transfers between devices, local(): lax.all_to_all(ordered, 'wave', split_axis=0, concat_axis=0, tiled=True)  4.26 us
    pallas_call x1, Pallas kernels, local(): pl.pallas_call(functools.partial(place_kernel, step, step_pad, rows_dev,...  2.78 us
    all_to_all x1, waiting for transfers between devices, local(): lax.all_to_all(ordered, 'wave', split_axis=0, concat_axis=0, tiled=True)  2.18 us
    select_n x2, other arithmetic, local(): ordered = jnp.take(fourier, lat_order, axis=0)  1.41 us
    reshape x1, local copies, waits for them, and re-layouts, local(): fourier = fourier.reshape(blocks, 2 * half_cycles, parts, block)  1.07 us
  transfers between devices with their start and end apart: 1, of which 1 were waited for; matrix products, arithmetic and copies ran while one was open for 5% of the time, Pallas kernels for 0%

profile of v1, /device:TPU:0, one launch (start us, length us, event | category | flops | bytes accessed | tf_op | source)
XLA Modules:
  0.0 46.8 jit_solution(5706364789255243230)
XLA Ops:
  0.0 0.7 %compare_select_fusion = s32[12]{0:T(128)S(1)} fusion(s32[12]{0:T(128)} %param.9), kind=kLoop, calls=%fused_computation.5 | loop fusion | flops 36 | bytes 96 | tf_op jit(solution)/shard_map/jit(_take)/jit(_where)/select_n | solution.py:205
  0.7 0.7 %compare_and_fusion = pred[12]{0:T(512)(128)(4,1)S(1)} fusion(s32[12]{0:T(128)} %param.9), kind=kLoop, calls=%fused_computation.10 | loop fusion | flops 72 | bytes 60 | tf_op jit(solution)/shard_map/jit(_take)/and | solution.py:205
  1.3 0.8 %dynamic_slice.3 = s32[320]{0:T(512)S(1)} dynamic-slice(s32[1280]{0:T(1024)} %param.7, s32[]{:T(128)S(6)} %select_n.61), dynamic_slice_sizes={320} | dynamic-slice | bytes 2564 | tf_op jit(solution)/shard_map/dynamic_slice | solution.py:187
  2.1 0.9 %reshape.85.wave_ref = s32[10,32,1]{2,1,0:T(8,128)} reshape(s32[320]{0:T(512)S(1)} %dynamic_slice.3) | data formatting | bytes 2560 | tf_op jit(solution)/shard_map/reshape | solution.py:202
  3.0 0.0 copy-start
  3.0 10.1 %legendre.1 = f32[10,2,6,192]{3,2,1,0:T(8,128)} custom-call(s32[10,32,1]{2,1,0:T(8,128)} %reshape.85.wave_ref, bf16[6,320,1280]{2,1,0:T(8,128)(2,1)} %bitcast.6, bf16[6,320,1280]{2,1,0:T(8,128)(2,1)} %bitcast.7), custom_call_target="tpu_custom_call" | custom-call | tf_op jit(solution)/shard_map/legendre/pallas_call | solution.py:191
  13.1 0.0 copy-start.2
  13.1 0.0 copy-start.1
  13.1 1.1 %reshape.65 = f32[10,12,6,32]{3,2,1,0:T(8,128)S(1)} reshape(f32[10,2,6,192]{3,2,1,0:T(8,128)} %legendre.1) | data formatting | bytes 184320 | tf_op jit(solution)/shard_map/reshape | solution.py:203
  14.2 0.2 copy.13
  14.4 0.2 reshape.66
  14.6 0.6 %gather_fusion.1 = f32[12,1920]{1,0:T(8,128)S(1)} fusion(f32[12,1920]{1,0:T(8,128)S(1)} %reshape.66, s32[1024]{0:T(1024)S(1)} %pad_clamp_fusion), kind=kCustom, calls=%fused_computation.1 | custom fusion | bytes 184368 | tf_op jit(solution)/shard_map/jit(_take)/gather | solution.py:205
  15.2 0.1 gather.12
  15.3 0.1 broadcast_in_dim.37
  15.4 0.7 %broadcast_select_fusion = f32[4,3,6,320]{3,2,1,0:T(8,128)} fusion(f32[4,3,6,320]{3,2,1,0:T(8,128)S(1)} %gather.12, pred[4,3]{1,0:T(4,128)(4,1)S(1)} %broadcast_in_dim.37), kind=kLoop, calls=%fused_computation.2 | loop fusion | flops 23040 | bytes 184332 | tf_op jit(solution)/shard_map/jit(_take)/select_n | solution.py:205
  16.1 4.3 %all-to-all-start = ((f32[4,3,6,320]{3,2,1,0:T(8,128)}), f32[4,3,6,320]{3,2,1,0:T(8,128)S(1)}, u32[]{:S(2)}, u32[]{:S(2)}) async-start(f32[4,3,6,320]{3,2,1,0:T(8,128)} %broadcast_select_fusion), calls=%async_computation | async-start | bytes 294912 | tf_op jit(solution)/shard_map/all_to_all | solution.py:207
  20.4 0.0 copy-done
  20.4 0.6 %gather_fusion = s32[3]{0:T(128)S(1)} fusion(s32[12]{0:T(128)S(1)} %copy-done, s32[1024]{0:T(1024)S(1)} %pad_clamp_fusion.1), kind=kCustom, calls=%fused_computation | custom fusion | bytes 36 | tf_op jit(solution)/shard_map/jit(_take)/gather | solution.py:211
  21.1 0.0 copy-done.2
  21.1 0.2 select_reduce_fusion
  21.3 0.5 %broadcast_divide_fusion.inv_ref = f32[3]{0:T(128)} fusion(s32[3]{0:T(128)S(1)} %select_reduce_fusion), kind=kLoop, calls=%fused_computation.14 | loop fusion | flops 6 | bytes 24 | tf_op jit(solution)/shard_map/div | solution.py:231
  21.8 0.6 %convert_element_type.6.len_ref = f32[3]{0:T(128)} convert(s32[3]{0:T(128)S(1)} %select_reduce_fusion) | non-fusion elementwise | flops 3 | bytes 24 | tf_op jit(solution)/shard_map/convert_element_type | solution.py:213
  22.4 0.0 copy-done.1
  22.4 0.6 %broadcast_in_dim.36.wave_ref = f32[1,1280]{1,0:T(1,128)} reshape(f32[1280]{0:T(1024)S(1)} %convert_element_type.7) | data formatting | bytes 10240 | tf_op jit(solution)/shard_map/broadcast_in_dim | solution.py:214
  23.0 2.2 %all-to-all-done = f32[4,3,6,320]{3,2,1,0:T(8,128)S(1)} async-done(((f32[4,3,6,320]{3,2,1,0:T(8,128)}), f32[4,3,6,320]{3,2,1,0:T(8,128)S(1)}, u32[]{:S(2)}, u32[]{:S(2)}) %all-to-all-start) | async-done | bytes 92192 | tf_op jit(solution)/shard_map/all_to_all | solution.py:207
  25.2 0.8 %reshape.67.coef_ref = f32[3,6,1280]{2,1,0:T(8,128)} reshape(f32[3,6,4,320]{3,2,1,0:T(4,128)S(1)} %copy.14) | data formatting | bytes 184320 | tf_op jit(solution)/shard_map/reshape | solution.py:208
  26.0 7.0 %synth.1.x_ref = f32[8,32,240]{2,1,0:T(8,128)} custom-call(f32[3]{0:T(128)} %convert_element_type.6.len_ref, f32[3]{0:T(128)} %broadcast_divide_fusion.inv_ref, f32[1,1280]{1,0:T(1,128)} %broadcast_in_dim.36.wave_ref, f32[3,6,1280]{2,1,0:T(8,128)} %reshape.67.coef_ref), custom_call_target="tpu_custom_call" | custom-call | tf_op jit(solution)/shard_map/synth/pallas_call | solution.py:220
  33.0 11.1 %exchange.1.x_ref = f32[8,32,240]{2,1,0:T(8,128)} custom-call(f32[8,32,240]{2,1,0:T(8,128)} %synth.1.x_ref), custom_call_target="tpu_custom_call" | custom-call | tf_op jit(solution)/shard_map/exchange/pallas_call | solution.py:232
  44.0 2.8 %place.1 = f32[3,15552]{1,0:T(4,128)} custom-call(f32[8,32,240]{2,1,0:T(8,128)} %exchange.1.x_ref), custom_call_target="tpu_custom_call" | custom-call | tf_op jit(solution)/shard_map/place/pallas_call | solution.py:245
  (6 shorter events, 0.1 us)
Async XLA Ops:
  3.0 17.5 %copy-start = (s32[12]{0:T(128)S(1)}, s32[12]{0:T(128)}, u32[]{:S(2)}) copy-start(s32[12]{0:T(128)} %param.9) | copy-start | bytes 148
  13.1 8.0 %copy-start.2 = (s32[6]{0:T(128)S(1)}, s32[6]{0:T(128)}, u32[]{:S(2)}) copy-start(s32[6]{0:T(128)} %param.8) | copy-start | bytes 76
  13.1 9.3 %copy-start.1 = (s32[1280]{0:T(1024)S(1)}, s32[1280]{0:T(1024)}, u32[]{:S(2)}) copy-start(s32[1280]{0:T(1024)} %param.7) | copy-start | bytes 15364
  16.1 9.0 %all-to-all-start = ((f32[4,3,6,320]{3,2,1,0:T(8,128)}), f32[4,3,6,320]{3,2,1,0:T(8,128)S(1)}, u32[]{:S(2)}, u32[]{:S(2)}) async-start(f32[4,3,6,320]{3,2,1,0:T(8,128)} %broadcast_select_fusion), calls=%async_computation | async-start | bytes 294912 | tf_op jit(solution)/shard_map/all_to_all | solution.py:207

commit v2 on v1

v2 whole, which is shorter than its diff:
```python
import functools
import math

import jax
import jax.numpy as jnp
from jax import lax
from jax.experimental import pallas as pl
from jax.experimental.pallas import tpu as pltpu
from jax.sharding import PartitionSpec as P

RMAX = 5136
FIELDS = 3


def split(value):
    high = value.astype(jnp.bfloat16)
    return high, (value - high.astype(jnp.float32)).astype(jnp.bfloat16)


def dot_nt(left, right):
    return lax.dot_general(left, right, (((1,), (1,)), ((), ())), preferred_element_type=jnp.float32)


def turns(t):
    y = math.pi * t
    z = y * y
    sine = jnp.full_like(z, 1.0 / math.factorial(13))
    for n in (11, 9, 7, 5, 3, 1):
        sign = -1.0 if (n // 2) % 2 else 1.0
        sine = sine * z + sign / math.factorial(n)
    sine = sine * y
    cosine = jnp.full_like(z, 1.0 / math.factorial(12))
    for n in (10, 8, 6, 4, 2, 0):
        sign = -1.0 if (n // 2) % 2 else 1.0
        cosine = cosine * z + sign / math.factorial(n)
    return 1.0 - 2.0 * sine * sine, 2.0 * sine * cosine


def points_kernel(
    step, step_pad, wave_ref, lat_ref, cycle_ref, coef_ref, out_ref,
    e_ref, w_ref, t_ref, place_ref, send_ref, got_ref, own_sem, send_sem, recv_sem,
):
    cycles, lev_count, rows_dev, wide = send_ref.shape
    parts, slots = coef_ref.shape[1:]
    fields = parts // 2
    half_cycles = cycle_ref.shape[0]
    me = lax.axis_index("lev")
    first_row = lax.axis_index("wave") * cycles
    barrier = pltpu.get_barrier_semaphore()
    for offset in range(1, lev_count):
        peer = lax.rem(me + offset, lev_count)
        pl.semaphore_signal(barrier, inc=1, device_id={"lev": peer}, device_id_type=pl.DeviceIdType.MESH)

    waves = wave_ref[...].astype(jnp.float32)
    weights = jnp.where(waves == 0.0, 1.0, 2.0)
    steps_e = (step_pad // 8 + 7) // 8 * 8
    steps_t = (lev_count + 7) // 8 * 8
    at_t = 8 + steps_e
    at_d = at_t + 8
    index = lax.broadcasted_iota(jnp.int32, (at_d + steps_t, 1), 0)
    mult = jnp.where(
        index < 8,
        index,
        jnp.where(index < at_t, 8 * (index - 8), jnp.where(index < at_d, step * (index - at_t), 8 * step * (index - at_d))),
    ).astype(jnp.float32)
    products = waves * mult
    copies = []
    for r in range(cycles):
        length = cycle_ref[lat_ref[first_row + r] % half_cycles].astype(jnp.float32)
        inverse = 1.0 / jnp.full((1, slots), length)
        whole = jnp.floor(products * inverse + 0.5)
        cosine, sine = turns((products - whole * length) * inverse)
        for k in range(step_pad // 8):
            c0, s0, c1, s1 = cosine[0:8], sine[0:8], cosine[8 + k : 9 + k], sine[8 + k : 9 + k]
            e_ref[0, 8 * k : 8 * k + 8] = c0 * c1 - s0 * s1
            e_ref[1, 8 * k : 8 * k + 8] = s0 * c1 + c0 * s1
        for k in range((lev_count + 1) // 2):
            tc, ts = [], []
            for d in (2 * k, 2 * k + 1):
                c0, s0 = cosine[at_t : at_d], sine[at_t : at_d]
                c1, s1 = cosine[at_d + d : at_d + d + 1], sine[at_d + d : at_d + d + 1]
                tc.append(c0 * c1 - s0 * s1)
                ts.append(s0 * c1 + c0 * s1)
            for place, value in ((0, tc), (slots, ts)):
                high, low = split(jnp.concatenate(value, axis=0))
                t_ref[0, 16 * k : 16 * k + 16, place : place + slots] = high
                t_ref[1, 16 * k : 16 * k + 16, place : place + slots] = low
        for f in range(fields):
            real = coef_ref[r, 2 * f : 2 * f + 1] * weights
            imag = coef_ref[r, 2 * f + 1 : 2 * f + 2] * weights
            for k in range(step_pad // 16):
                ec = e_ref[0, 16 * k : 16 * k + 16]
                es = e_ref[1, 16 * k : 16 * k + 16]
                at = f * step_pad + 16 * k
                for place, value in ((0, real * ec - imag * es), (slots, -(real * es + imag * ec))):
                    high, low = split(value)
                    w_ref[0, at : at + 16, place : place + slots] = high
                    w_ref[1, at : at + 16, place : place + slots] = low
        total = dot_nt(t_ref[0], w_ref[0]) + dot_nt(t_ref[0], w_ref[1]) + dot_nt(t_ref[1], w_ref[0])
        shape = total.shape
        point = lax.broadcasted_iota(jnp.int32, shape, 0) * step + lax.broadcasted_iota(jnp.int32, shape, 1) % step_pad
        total = jnp.where(point.astype(jnp.float32) < length, total, 0.0)[: lev_count * rows_dev]
        pieces = [total[:, f * step_pad : f * step_pad + step] for f in range(fields)]
        if wide > fields * step:
            pieces.append(jnp.zeros((lev_count * rows_dev, wide - fields * step), jnp.float32))
        send_ref[r] = jnp.concatenate(pieces, axis=1).reshape(lev_count, rows_dev, wide)
        if r == 0:
            pl.semaphore_wait(barrier, lev_count - 1)
        started = []
        for offset in range(1, lev_count):
            peer = lax.rem(me + offset, lev_count)
            copy = pltpu.make_async_remote_copy(
                src_ref=send_ref.at[r, peer],
                dst_ref=got_ref.at[r, me],
                send_sem=send_sem.at[r, offset],
                recv_sem=recv_sem.at[r, offset],
                device_id={"lev": peer},
                device_id_type=pl.DeviceIdType.MESH,
            )
            copy.start()
            started.append(copy)
        kept = pltpu.make_async_copy(send_ref.at[r, me], got_ref.at[r, me], own_sem.at[r])
        kept.start()
        started.append(kept)
        copies.append(started)

    group = lev_count * fields
    span = step * group
    source = lax.broadcasted_iota(jnp.int32, (wide, 1), 0)
    target = jnp.where(source < fields * step, (source % step) * group + source // step, -1)
    lane = lax.broadcasted_iota(jnp.int32, place_ref.shape, 1)
    place_ref[...] = jnp.where(lane == target, 1.0, 0.0).astype(jnp.bfloat16)
    for r in range(cycles):
        for copy in copies[r]:
            copy.wait()
        high, low = split(got_ref[r].reshape(lev_count * rows_dev, wide))
        spread = jnp.dot(high, place_ref[...], preferred_element_type=jnp.float32) + jnp.dot(
            low, place_ref[...], preferred_element_type=jnp.float32
        )
        total = spread[:rows_dev]
        for level in range(1, lev_count):
            total = total + pltpu.roll(spread[level * rows_dev : (level + 1) * rows_dev], fields * level, 1)
        for q in range(rows_dev):
            out_ref[r : r + 1, q * span : (q + 1) * span] = total[q : q + 1, :span]


def legendre_kernel(wave_ref, spec_ref, leg_ref, out_ref):
    parts, block, degrees = spec_ref.shape
    half_cycles = leg_ref.shape[0]
    table = leg_ref[...].reshape(half_cycles * block, degrees)
    waves = wave_ref[0]
    degree = lax.broadcasted_iota(jnp.int32, (block, degrees), 1)
    live = degree >= waves
    parity = (degree + waves) & 1
    values = spec_ref[...]
    cells = parts * block
    shape = (half_cycles, block, cells)
    own = lax.broadcasted_iota(jnp.int32, shape, 1) == lax.broadcasted_iota(jnp.int32, shape, 2) % block
    sums = []
    for which in (0, 1):
        mask = jnp.where(live & (parity == which), 1.0, 0.0).astype(jnp.bfloat16)
        part = (values * mask[None]).reshape(cells, degrees)
        product = dot_nt(table, part).reshape(shape)
        sums.append(jnp.sum(jnp.where(own, product, 0.0), axis=1))
    out_ref[0, 0] = sums[0] + sums[1]
    out_ref[0, 1] = sums[0] - sums[1]


def local(spectral, legendre, slot_wave, cycle_len, lat_order):
    slot_count = spectral.shape[2]
    degrees = spectral.shape[3]
    half_cycles = legendre.shape[1]
    wave_index = lax.axis_index("wave")
    lev_count = lax.axis_size("lev")
    wave_count = lax.axis_size("wave")
    slots = slot_wave.shape[0]
    padded_len = (RMAX + 8 * lev_count - 1) // (8 * lev_count) * 8 * lev_count
    points_dev = padded_len // lev_count
    step = points_dev // 8
    step_pad = (step + 15) // 16 * 16
    parts = spectral.shape[0] * spectral.shape[1]
    cycle_count = lat_order.shape[0] // wave_count

    local_waves = lax.dynamic_slice_in_dim(slot_wave, wave_index * slot_count, slot_count)
    block = 32 if slot_count % 32 == 0 else 16
    blocks = slot_count // block
    cells = parts * block
    fourier = pl.pallas_call(
        legendre_kernel,
        grid=(blocks,),
        out_shape=jax.ShapeDtypeStruct((blocks, 2, half_cycles, cells), jnp.float32),
        in_specs=[
            pl.BlockSpec((1, block, 1), lambda i: (i, 0, 0)),
            pl.BlockSpec((parts, block, degrees), lambda i: (0, i, 0)),
            pl.BlockSpec((half_cycles, block, degrees), lambda i: (0, i, 0)),
        ],
        out_specs=pl.BlockSpec((1, 2, half_cycles, cells), lambda i: (i, 0, 0, 0)),
        name="legendre",
    )(local_waves.reshape(blocks, block, 1), spectral.reshape(parts, slot_count, degrees), jnp.transpose(legendre, (1, 0, 2)))
    fourier = fourier.reshape(blocks, 2 * half_cycles, parts, block)
    fourier = jnp.transpose(fourier, (1, 2, 0, 3)).reshape(2 * half_cycles, parts * slot_count)
    ordered = jnp.take(fourier, lat_order, axis=0, mode="clip")
    ordered = ordered.reshape(wave_count, cycle_count, parts, slot_count)
    shared = lax.all_to_all(ordered, "wave", split_axis=0, concat_axis=0, tiled=True)
    coeffs = jnp.transpose(shared, (1, 2, 0, 3)).reshape(cycle_count, parts, slots)

    wide = (parts // 2 * step + 127) // 128 * 128
    span = (parts // 2 * lev_count * step + 127) // 128 * 128
    smem = pl.BlockSpec(memory_space=pltpu.SMEM)
    vmem = pl.BlockSpec(memory_space=pltpu.VMEM)
    row_pad = (lev_count + 1) // 2 * 16
    return pl.pallas_call(
        functools.partial(points_kernel, step, step_pad),
        out_shape=jax.ShapeDtypeStruct((cycle_count, points_dev * lev_count * (parts // 2)), jnp.float32),
        in_specs=[vmem, smem, smem, vmem],
        out_specs=vmem,
        scratch_shapes=[
            pltpu.VMEM((2, step_pad, slots), jnp.float32),
            pltpu.VMEM((2, parts // 2 * step_pad, 2 * slots), jnp.bfloat16),
            pltpu.VMEM((2, row_pad, 2 * slots), jnp.bfloat16),
            pltpu.VMEM((wide, span), jnp.bfloat16),
            pltpu.VMEM((cycle_count, lev_count, 8, wide), jnp.float32),
            pltpu.VMEM((cycle_count, lev_count, 8, wide), jnp.float32),
            pltpu.SemaphoreType.DMA((cycle_count,)),
            pltpu.SemaphoreType.DMA((cycle_count, lev_count)),
            pltpu.SemaphoreType.DMA((cycle_count, lev_count)),
        ],
        compiler_params=pltpu.CompilerParams(collective_id=0, has_side_effects=True),
        name="points",
    )(slot_wave[None, :], lat_order, cycle_len, coeffs)


def solution(mesh):
    in_specs = (P("lev", None, "wave", None), P("wave", None, None), P(), P(), P())
    out_specs = P("wave", "lev")
    return jax.shard_map(local, mesh=mesh, in_specs=in_specs, out_specs=out_specs, check_vma=False)
```

time: 47.4 us -> 45.8 us (0.966)
  other arithmetic: 3.4 us -> 0.01 us
  waiting for transfers between devices: 2.18 us -> 4.18 us
  Pallas kernels: 31 us -> 29.2 us
  local copies, waits for them, and re-layouts: 5.94 us -> 7.53 us
    all_to_all x1, waiting for transfers between devices: 2.18 us -> 4.18 us  [local(): lax.all_to_all(ordered, 'wave', split_axis=0, concat_axis=0, tiled=True)]
    pallas_call x3 -> x1, Pallas kernels: 20.8 us -> 19 us  [local(): pl.pallas_call(functools.partial(points_kernel, step, step_pad), out_shap...]
    unnamed x6 -> x5, local copies, waits for them, and re-layouts: 0.01 us -> 1.69 us
    select_n x4 -> x0, other arithmetic: 1.43 us -> none  [the longest x2 1.41 us: local(): ordered = jnp.take(fourier, lat_order, axis=0)]
    reshape x0 -> x1, local copies, waits for them, and re-layouts: none -> 0.75 us  [local(): ordered = ordered.reshape(wave_count, cycle_count, parts, slot_count)]
    gather x3 -> x1, local copies, waits for them, and re-layouts: 1.33 us -> 0.59 us  [local(): ordered = jnp.take(fourier, lat_order, axis=0, mode='clip')]
    and x1 -> x0, other arithmetic: 0.66 us -> none  [local(): ordered = jnp.take(fourier, lat_order, axis=0)]
    convert_element_type x2 -> x0, other arithmetic: 0.59 us -> none  [the longest x1 0.59 us: local(): jnp.sum(jnp.where(pair_match, cycle_len[None, :], 0), axis=1)]
  transfers between devices with their start and end apart: 1 -> 1, of which waited for: 1 -> 1; matrix products, arithmetic and copies ran while one was open for 5% -> 1% of each run, Pallas kernels for 0% -> 0%
where the time goes in v2:
time: 45.8 us; the launch traced here: 45.2 us
  Pallas kernels  29.2 us (64%)
  local copies, waits for them, and re-layouts  7.53 us (16%)
  starting transfers between devices  4.27 us (9%)
  waiting for transfers between devices  4.18 us (9%)
    pallas_call x1, Pallas kernels, local(): pl.pallas_call(functools.partial(points_kernel, step, step_pad), out_shap...  19 us
    pallas_call x1, Pallas kernels, local(): pl.pallas_call(legendre_kernel, grid=(blocks,), out_shape=jax.ShapeDtypeS...  10.2 us
    all_to_all x1, starting transfers between devices, local(): lax.all_to_all(ordered, 'wave', split_axis=0, concat_axis=0, tiled=True)  4.27 us
    all_to_all x1, waiting for transfers between devices, local(): lax.all_to_all(ordered, 'wave', split_axis=0, concat_axis=0, tiled=True)  4.18 us
    unnamed x5, local copies, waits for them, and re-layouts  1.69 us
    reshape x1, local copies, waits for them, and re-layouts, local(): fourier = fourier.reshape(blocks, 2 * half_cycles, parts, block)  1.04 us
  transfers between devices with their start and end apart: 1, of which 1 were waited for; matrix products, arithmetic and copies ran while one was open for 1% of the time, Pallas kernels for 0%

profile of v2, /device:TPU:0, one launch (start us, length us, event | category | flops | bytes accessed | tf_op | source)
XLA Modules:
  0.0 45.2 jit_solution(4006130793527475525)
XLA Ops:
  0.0 0.8 %dynamic_slice.3 = s32[320]{0:T(512)S(1)} dynamic-slice(s32[1280]{0:T(1024)} %param.7, s32[]{:T(128)S(6)} %select_n.3), dynamic_slice_sizes={320} | dynamic-slice | bytes 2564 | tf_op jit(solution)/shard_map/dynamic_slice | solution.py:184
  0.8 0.9 %reshape.33.wave_ref = s32[10,32,1]{2,1,0:T(8,128)} reshape(s32[320]{0:T(512)S(1)} %dynamic_slice.3) | data formatting | bytes 2560 | tf_op jit(solution)/shard_map/reshape | solution.py:199
  1.6 0.0 copy-start.1
  1.6 0.0 copy-start
  1.7 10.2 %legendre.1 = f32[10,2,6,192]{3,2,1,0:T(8,128)} custom-call(s32[10,32,1]{2,1,0:T(8,128)} %reshape.33.wave_ref, bf16[6,320,1280]{2,1,0:T(8,128)(2,1)} %bitcast.4, bf16[6,320,1280]{2,1,0:T(8,128)(2,1)} %bitcast.5), custom_call_target="tpu_custom_call" | custom-call | tf_op jit(solution)/shard_map/legendre/pallas_call | solution.py:188
  11.8 1.0 %reshape.20 = f32[10,12,6,32]{3,2,1,0:T(8,128)S(1)} reshape(f32[10,2,6,192]{3,2,1,0:T(8,128)} %legendre.1) | data formatting | bytes 184320 | tf_op jit(solution)/shard_map/reshape | solution.py:200
  12.9 0.2 copy.9
  13.1 0.2 reshape.21
  13.3 0.0 copy-done.1
  13.3 0.6 %gather_fusion = f32[12,1920]{1,0:T(8,128)S(1)} fusion(f32[12,1920]{1,0:T(8,128)S(1)} %reshape.21, s32[1024]{0:T(1024)S(1)} %pad_clamp_fusion), kind=kCustom, calls=%fused_computation | custom fusion | bytes 184368 | tf_op jit(solution)/shard_map/jit(_take)/gather | solution.py:202
  13.9 0.8 %reshape.22 = f32[4,3,6,320]{3,2,1,0:T(8,128)} reshape(f32[12,1920]{1,0:T(8,128)S(1)} %gather_fusion) | data formatting | bytes 184320 | tf_op jit(solution)/shard_map/reshape | solution.py:203
  14.7 4.3 %all-to-all-start = ((f32[4,3,6,320]{3,2,1,0:T(8,128)}), f32[4,3,6,320]{3,2,1,0:T(8,128)S(1)}, u32[]{:S(2)}, u32[]{:S(2)}) async-start(f32[4,3,6,320]{3,2,1,0:T(8,128)} %reshape.22), calls=%async_computation | async-start | bytes 294912 | tf_op jit(solution)/shard_map/all_to_all | solution.py:204
  18.9 0.0 copy-done
  18.9 0.6 %broadcast_in_dim.7.wave_ref = s32[1,1280]{1,0:T(1,128)} reshape(s32[1280]{0:T(1024)S(1)} %copy-done) | data formatting | bytes 10240 | tf_op jit(solution)/shard_map/broadcast_in_dim | solution.py:230
  19.5 4.2 %all-to-all-done = f32[4,3,6,320]{3,2,1,0:T(8,128)S(1)} async-done(((f32[4,3,6,320]{3,2,1,0:T(8,128)}), f32[4,3,6,320]{3,2,1,0:T(8,128)S(1)}, u32[]{:S(2)}, u32[]{:S(2)}) %all-to-all-start) | async-done | bytes 92192 | tf_op jit(solution)/shard_map/all_to_all | solution.py:204
  23.7 0.8 %reshape.23.coef_ref = f32[3,6,1280]{2,1,0:T(8,128)} reshape(f32[3,6,4,320]{3,2,1,0:T(4,128)S(1)} %copy.10) | data formatting | bytes 184320 | tf_op jit(solution)/shard_map/reshape | solution.py:205
  24.5 19.0 %points.1 = f32[3,15552]{1,0:T(4,128)} custom-call(s32[1,1280]{1,0:T(1,128)} %broadcast_in_dim.7.wave_ref, s32[12]{0:T(128)} %lat_ref.1, s32[6]{0:T(128)} %cycle_ref.1, f32[3,6,1280]{2,1,0:T(8,128)} %reshape.23.coef_ref), custom_call_target="tpu_custom_call" | custom-call | tf_op jit(solution)/shard_map/points/pallas_call | solution.py:212
  43.5 1.7 %copy.12 = f32[3,15552]{1,0:T(4,128)} copy(f32[3,15552]{1,0:T(4,128)} %points.1) | data formatting | bytes 373248
  (2 shorter events, 0.0 us)
Async XLA Ops:
  1.6 11.6 %copy-start.1 = (s32[12]{0:T(128)S(1)}, s32[12]{0:T(128)}, u32[]{:S(2)}) copy-start(s32[12]{0:T(128)} %lat_ref.1) | copy-start | bytes 148
  1.6 17.3 %copy-start = (s32[1280]{0:T(1024)S(1)}, s32[1280]{0:T(1024)}, u32[]{:S(2)}) copy-start(s32[1280]{0:T(1024)} %param.7) | copy-start | bytes 15364
  14.7 9.0 %all-to-all-start = ((f32[4,3,6,320]{3,2,1,0:T(8,128)}), f32[4,3,6,320]{3,2,1,0:T(8,128)S(1)}, u32[]{:S(2)}, u32[]{:S(2)}) async-start(f32[4,3,6,320]{3,2,1,0:T(8,128)} %reshape.22), calls=%async_computation | async-start | bytes 294912 | tf_op jit(solution)/shard_map/all_to_all | solution.py:204
